TPU v7x, 128 devices: a whole 4x4x4 slice. The times are simulated.
128 devices in a mesh: wide: 32 (over z, y_hi, x), narrow: 4 (over y_lo, core).
Axes of the slice: x: 4, y: 4 (y_hi: 2, y_lo: 2; y = y_hi * 2 + y_lo), z: 4, core: 2. Of those that a mesh axis runs over, the one named last changes fastest.
Arguments:
- spectra: bfloat16 [2, 128, 64, 32, 256], P(None, ('wide', 'narrow')), may hold values from -6 to 6
- out_grads: bfloat16 [2, 128, 64, 32, 256], P(None, ('wide', 'narrow')), may hold values from -0.375 to 0.375
- weights: float32 [2, 64, 32, 256, 256], P(None, 'wide', 'narrow'), may hold values from -6 to 6
- mode_factor: float32 [64, 8], replicated, may hold values from -2 to 2
- in_factor: float32 [256, 64], replicated, may hold values from -0.75 to 0.75
- out_factor: float32 [256, 64], replicated, may hold values from -0.75 to 0.75
- first_moment: float32 [2, 8, 32, 4096], P(None, None, 'narrow', 'wide'), may hold values from -60 to 60
- second_moment: float32 [8, 32, 4096], P(None, 'narrow', 'wide'), may hold values from 20 to 500
Outputs:
- new_weights: float32 [2, 64, 32, 256, 256], P(None, 'wide', 'narrow')
- new_first: float32 [2, 8, 32, 4096], P(None, None, 'narrow', 'wide')
- new_second: float32 [8, 32, 4096], P(None, 'narrow', 'wide')
All inputs are finite; a program needn't handle non-finite values.
Results may differ from a plain program's by a relative error of at most 0.0003.
Values may be sent and summed in bfloat16 or wider, within the bound.
No kernel may reach another device: no remote copies, remote signals or barrier semaphores. Data moves between devices by JAX's collectives and lax.ppermute only.
A program may use at most 128 MiB of HBM per device.

v0:
```python
import jax
import jax.numpy as jnp
from jax import lax
from jax.sharding import PartitionSpec as P

STEP = 1000
highest = lax.Precision.HIGHEST


def local(
    spectra, out_grads, weights, mode_factor, in_factor, out_factor, first_moment, second_moment
):
    wide_count = lax.axis_size("wide")
    narrow_count = lax.axis_size("narrow")
    modes_first = spectra.shape[2]
    modes_second = spectra.shape[3]
    channels = spectra.shape[4]
    first_mine = modes_first // wide_count
    second_mine = modes_second // narrow_count
    local_modes = first_mine * second_mine
    rank_in = in_factor.shape[1]
    rank_out = out_factor.shape[1]

    def arrange(source):
        sample_rows = source.shape[1]
        width = source.shape[4]
        source = source.reshape(
            2, sample_rows, wide_count, first_mine, narrow_count, second_mine, width
        )
        source = source.transpose(0, 1, 2, 4, 3, 5, 6)
        return source.reshape(2, sample_rows, wide_count * narrow_count * local_modes, width)

    mine_spectra, mine_grads = (
        lax.all_to_all(
            arrange(spectra), ("wide", "narrow"), split_axis=2, concat_axis=1, tiled=True
        ),
        lax.all_to_all(
            arrange(out_grads), ("wide", "narrow"), split_axis=2, concat_axis=1, tiled=True
        ),
    )
    products = jnp.einsum(
        "pbmi,qbmo->pqmio", mine_spectra, mine_grads, preferred_element_type=jnp.float32
    )
    grad = jnp.stack([products[0, 0] + products[1, 1], products[0, 1] - products[1, 0]])
    half_core = jnp.einsum("pmio,oc->pmic", grad, out_factor, precision=highest)
    channel_core = jnp.einsum("ia,pmic->pmac", in_factor, half_core, precision=highest)
    channel_core = channel_core.reshape(2, first_mine, second_mine, rank_in * rank_out)
    wide_position = lax.axis_index("wide")
    mine_rows = lax.dynamic_slice_in_dim(mode_factor, wide_position * first_mine, first_mine, 0)
    partial_core = jnp.einsum("xr,pxmk->prmk", mine_rows, channel_core, precision=highest)
    core_grad = lax.psum_scatter(partial_core, "wide", scatter_dimension=3, tiled=True)
    new_first = 0.9 * first_moment + 0.1 * core_grad
    new_second = 0.999 * second_moment + 0.001 * (
        core_grad[0] * core_grad[0] + core_grad[1] * core_grad[1]
    )
    first_scale = 1.0 / (1.0 - 0.9**STEP)
    second_scale = 1.0 / (1.0 - 0.999**STEP)
    core_step = new_first * first_scale / (jnp.sqrt(new_second * second_scale) + 1e-08)
    expanded = jnp.einsum(
        "xr,prmk->pxmk",
        mine_rows,
        lax.all_gather(core_step, "wide", axis=3, tiled=True),
        precision=highest,
    )
    expanded = expanded.reshape(2, local_modes, rank_in, rank_out)
    left_part = jnp.einsum("pmac,oc->pmao", expanded, out_factor, precision=highest)
    change = jnp.einsum("ia,pmao->pmio", in_factor, left_part, precision=highest)
    change = change.reshape(2, first_mine, second_mine, channels, channels)
    new_weights = weights - 0.3 * change
    return (new_weights, new_first, new_second)


def solution(mesh):
    placed = (
        P(None, ("wide", "narrow"), None, None, None),
        P(None, ("wide", "narrow"), None, None, None),
        P(None, "wide", "narrow", None, None),
        P(),
        P(),
        P(),
        P(None, None, "narrow", "wide"),
        P(None, "narrow", "wide"),
    )
    return jax.shard_map(
        local,
        mesh=mesh,
        in_specs=placed,
        out_specs=(
            P(None, "wide", "narrow", None, None),
            P(None, None, "narrow", "wide"),
            P(None, "narrow", "wide"),
        ),
        check_vma=False,
    )
```

profile of v0, /device:TPU:0, one launch (start us, length us, event | category | flops | bytes accessed | tf_op | source)
XLA Modules:
  0.0 412.7 jit_solution(15778321747352976225)
XLA Ops:
  7.2 0.0 copy-start
  7.2 1.8 copy.52
  9.0 14.0 %copy.53 = bf16[2,1,2048,256]{3,0,1,2:T(2,128)(2,1)} copy(bf16[2,1,2048,256]{3,2,0,1:T(8,128)(2,1)S(1)} %bitcast.77) | data formatting | bytes 4194304 | tf_op jit(solution)/shard_map/reshape | solution.py:31
  23.0 11.2 %all-to-all-start.1 = ((bf16[2,1,2048,256]{3,0,1,2:T(2,128)(2,1)}), bf16[2,1,2048,256]{3,0,1,2:T(2,128)(2,1)S(1)}, u32[]{:S(2)}, u32[]{:S(2)}) async-start(bf16[2,1,2048,256]{3,0,1,2:T(2,128)(2,1)} %copy.53), calls=%async_computation.1 | async-start | bytes 4194304 | tf_op jit(solution)/shard_map/all_to_all | solution.py:34
  34.2 1.8 copy.49
  36.0 14.0 %copy.50 = bf16[2,1,2048,256]{3,0,1,2:T(2,128)(2,1)} copy(bf16[2,1,2048,256]{3,2,0,1:T(8,128)(2,1)S(1)} %bitcast.78) | data formatting | bytes 4194304 | tf_op jit(solution)/shard_map/reshape | solution.py:31
  49.9 14.4 %all-to-all-done.1 = bf16[2,1,2048,256]{3,0,1,2:T(2,128)(2,1)S(1)} async-done(((bf16[2,1,2048,256]{3,0,1,2:T(2,128)(2,1)}), bf16[2,1,2048,256]{3,0,1,2:T(2,128)(2,1)S(1)}, u32[]{:S(2)}, u32[]{:S(2)}) %all-to-all-start.1) | async-done | bytes 2097184 | tf_op jit(solution)/shard_map/all_to_all | solution.py:34
  64.3 5.8 %all-to-all-start = ((bf16[2,1,2048,256]{3,0,1,2:T(2,128)(2,1)}), bf16[2,1,2048,256]{3,0,1,2:T(2,128)(2,1)}, u32[]{:S(2)}, u32[]{:S(2)}) async-start(bf16[2,1,2048,256]{3,0,1,2:T(2,128)(2,1)} %copy.50), calls=%async_computation | async-start | bytes 4194304 | tf_op jit(solution)/shard_map/all_to_all | solution.py:37
  70.1 0.2 reduce-scatter.2.cloned.1.call-start
  70.3 29.5 %all-to-all-done = bf16[2,1,2048,256]{3,0,1,2:T(2,128)(2,1)} async-done(((bf16[2,1,2048,256]{3,0,1,2:T(2,128)(2,1)}), bf16[2,1,2048,256]{3,0,1,2:T(2,128)(2,1)}, u32[]{:S(2)}, u32[]{:S(2)}) %all-to-all-start) | async-done | bytes 2097184 | tf_op jit(solution)/shard_map/all_to_all | solution.py:37
  99.8 7.4 %convolution_bitcast_fusion = f32[2,2,16,256,256]{3,4,0,1,2:T(8,128)S(1)} fusion(bf16[2,128,16,256,1]{3,0,2,1,4:T(2,128)(2,1)S(1)} %bitcast.76, bf16[2,128,16,256,1]{3,0,2,1,4:T(2,128)(2,1)} %bitcast.4), kind=kOutput, calls=%fused_computation | convolution fusion | flops 1073741824 | bytes 20971520 | tf_op jit(solution)/shard_map/pbmi,qbmo->pqmio/dot_general | solution.py:41
  107.2 0.6 fusion.4
  107.8 0.0 copy-start.1
  107.8 0.6 fusion.6
  108.4 0.2 copy-done.1
  108.6 5.6 %fusion = f32[2,16,256,64]{2,3,1,0:T(8,128)S(1)} fusion(f32[1,16,256,256]{2,3,1,0:T(8,128)S(1)} %fusion.4, f32[1,16,256,256]{2,3,1,0:T(8,128)S(1)} %fusion.6, f32[256,64]{0,1:T(8,128)S(1)} %copy-done.1), kind=kOutput, calls=%fused_computation.1 | convolution fusion | flops 1612709888 | bytes 10551296 | tf_op jit(solution)/shard_map/pmio,oc->pmic/dot_general | solution.py:45
  114.2 0.0 copy-done
  114.2 2.0 convolution_bitcast_fusion.3
  116.3 0.0 copy-start.4
  116.3 0.3 copy.60
  116.6 0.4 reshape.79
  117.0 0.0 copy-done.4
  117.0 0.0 copy-start.3
  117.0 0.0 copy-start.2
  117.0 3.5 convolution_bitcast_fusion.1
  120.5 0.0 reduce-scatter.2.cloned.1.call-update
  120.6 0.0 all-gather.2.cloned.1.call-start
  120.6 185.0 %reduce-scatter.2.cloned.1.call-done = f32[2,8,8,128]{3,1,2,0:T(8,128)} async-done(((f32[2,8,8,4096]{3,1,2,0:T(8,128)}), f32[2,8,8,128]{3,1,2,0:T(8,128)}) %reduce-scatter.2.cloned.1.call-update) | async-done | bytes 65552 | tf_op jit(solution)/shard_map/reduce_scatter | solution.py:51
  305.6 0.0 copy-done.3
  305.6 0.8 sqrt_add_fusion
  306.4 0.0 copy-done.2
  306.5 1.5 broadcast_divide_fusion
  307.9 0.0 all-gather.2.cloned.1.call-update
  308.0 0.6 copy.66
  308.6 0.6 copy.67
  309.2 62.1 %all-gather.2.cloned.1.call-done = f32[2,8,8,4096]{3,1,2,0:T(8,128)} async-done(((f32[2,8,8,128]{3,1,2,0:T(8,128)}), f32[2,8,8,4096]{3,1,2,0:T(8,128)}) %all-gather.2.cloned.1.call-update) | async-done | bytes 2097168 | tf_op jit(solution)/shard_map/all_gather | solution.py:62
  371.3 3.6 convolution_bitcast_fusion.2
  374.9 0.3 copy.64
  375.2 0.4 reshape.80
  375.6 1.9 fusion.12
  377.5 9.1 %broadcast_multiply_fusion = f32[2,16,256,256]{3,2,1,0:T(8,128)} fusion(f32[2,16,64,256]{3,2,1,0:T(8,128)S(1)} %fusion.12, f32[256,64]{0,1:T(8,128)S(1)} %copy-done), kind=kOutput, calls=%fused_computation.13 | convolution fusion | flops 1612709888 | bytes 10551296 | tf_op jit(solution)/shard_map/ia,pmao->pmio/dot_general | solution.py:67
  386.5 8.7 %copy.65 = f32[2,2,8,256,256]{4,3,2,1,0:T(8,128)} copy(f32[2,2,8,256,256]{3,4,2,1,0:T(8,128)} %bitcast.75) | data formatting | bytes 16777216 | tf_op jit(solution)/shard_map/mul | solution.py:69
  395.3 10.6 %sub.18 = f32[2,2,8,256,256]{4,3,2,1,0:T(8,128)} subtract(f32[2,2,8,256,256]{4,3,2,1,0:T(8,128)} %param.10, f32[2,2,8,256,256]{4,3,2,1,0:T(8,128)} %copy.65) | non-fusion elementwise | flops 2097152 | bytes 25165824 | tf_op jit(solution)/shard_map/sub | solution.py:69
Async XLA Ops:
  7.2 107.1 %copy-start = (f32[256,64]{0,1:T(8,128)S(1)}, f32[256,64]{0,1:T(8,128)}, u32[]{:S(2)}) copy-start(f32[256,64]{0,1:T(8,128)} %param.12) | copy-start | bytes 196612
  23.0 41.3 %all-to-all-start.1 = ((bf16[2,1,2048,256]{3,0,1,2:T(2,128)(2,1)}), bf16[2,1,2048,256]{3,0,1,2:T(2,128)(2,1)S(1)}, u32[]{:S(2)}, u32[]{:S(2)}) async-start(bf16[2,1,2048,256]{3,0,1,2:T(2,128)(2,1)} %copy.53), calls=%async_computation.1 | async-start | bytes 4194304 | tf_op jit(solution)/shard_map/all_to_all | solution.py:34
  64.3 35.5 %all-to-all-start = ((bf16[2,1,2048,256]{3,0,1,2:T(2,128)(2,1)}), bf16[2,1,2048,256]{3,0,1,2:T(2,128)(2,1)}, u32[]{:S(2)}, u32[]{:S(2)}) async-start(bf16[2,1,2048,256]{3,0,1,2:T(2,128)(2,1)} %copy.50), calls=%async_computation | async-start | bytes 4194304 | tf_op jit(solution)/shard_map/all_to_all | solution.py:37
  70.1 235.5 %reduce-scatter.2.cloned.1.call-start = ((), (), s32[]{:S(2)}) async-start(), calls=%async_computation.3 | async-start | bytes 2162688 | tf_op jit(solution)/shard_map/reduce_scatter | solution.py:51
  107.8 0.8 copy-start.1
  116.3 0.7 copy-start.4
  117.0 188.7 %copy-start.3 = (f32[8,8,128]{2,1,0:T(8,128)S(1)}, f32[8,8,128]{2,1,0:T(8,128)}, u32[]{:S(2)}) copy-start(f32[8,8,128]{2,1,0:T(8,128)} %param.15) | copy-start | bytes 98308
  117.0 189.5 %copy-start.2 = (f32[2,8,8,128]{3,2,1,0:T(8,128)S(1)}, f32[2,8,8,128]{3,2,1,0:T(8,128)}, u32[]{:S(2)}) copy-start(f32[2,8,8,128]{3,2,1,0:T(8,128)} %param.14) | copy-start | bytes 196612
  120.6 250.7 %all-gather.2.cloned.1.call-start = ((), (), s32[]{:S(2)}) async-start(), calls=%async_computation.4 | async-start | bytes 2162688 | tf_op jit(solution)/shard_map/all_gather | solution.py:62
Sparse Core Ops, SparseCore 0:
  120.7 184.9 reduce-scatter.1
  309.0 62.2 all-gather.1
where the time goes:
time: 413 us
  waiting for transfers between devices  291 us (70%)
  local copies, waits for them, and re-layouts  43.2 us (10%)
  matrix products  33 us (8%)
  starting transfers between devices  17.2 us (4%)
  between operations  14.2 us (3%)
  other arithmetic  14.1 us (3%)
    reduce_scatter x1, waiting for transfers between devices, local(): lax.psum_scatter(partial_core, 'wide', scatter_dimension=3, tiled=True)  185 us
    all_gather x1, waiting for transfers between devices, local(): lax.all_gather(core_step, 'wide', axis=3, tiled=True)  62.1 us
    all_to_all x1, waiting for transfers between devices, local(): lax.all_to_all(arrange(out_grads), ('wide', 'narrow'), split_axis=2, conc...  29.5 us
    reshape x2, local copies, waits for them, and re-layouts, arrange(): source.reshape(2, sample_rows, wide_count * narrow_count * local_modes, w...  28 us
    all_to_all x1, waiting for transfers between devices, local(): lax.all_to_all(arrange(spectra), ('wide', 'narrow'), split_axis=2, concat...  14.4 us
    all_to_all x1, starting transfers between devices, local(): lax.all_to_all(arrange(spectra), ('wide', 'narrow'), split_axis=2, concat...  11.2 us
    sub x1, other arithmetic, local(): new_weights = weights - 0.3 * change  10.6 us
    dot_general x1, matrix products, local(): jnp.einsum('ia,pmao->pmio', in_factor, left_part, precision=highest)  9.08 us
  transfers between devices with their start and end apart: 4, of which 4 were waited for; matrix products, arithmetic and copies ran while one was open for 4% of the time, Pallas kernels for 0%

commit v1 on v0

--- a/solution.py
+++ b/solution.py
@@ -59,7 +59,9 @@
     expanded = jnp.einsum(
         "xr,prmk->pxmk",
         mine_rows,
-        lax.all_gather(core_step, "wide", axis=3, tiled=True),
+        jnp.concatenate(
+            lax.all_to_all(jnp.stack([core_step] * lax.axis_size("wide")), "wide", 0, 0), axis=3
+        ),
         precision=highest,
     )
     expanded = expanded.reshape(2, local_modes, rank_in, rank_out)

time: 413 us -> 377 us (0.913)
  waiting for transfers between devices: 291 us -> 250 us
    all_gather x1 -> x0, waiting for transfers between devices: 62.1 us -> none  [local(): lax.all_gather(core_step, 'wide', axis=3, tiled=True)]
    all_to_all x0 -> x1, waiting for transfers between devices: none -> 18.1 us  [local(): lax.all_to_all(jnp.stack([core_step] * lax.axis_size('wide')), 'wide', 0, 0)]
  transfers between devices with their start and end apart: 4 -> 4, of which waited for: 4 -> 4; matrix products, arithmetic and copies ran while one was open for 4% -> 5% of each run, Pallas kernels for 0% -> 0%
where the time goes in v1:
time: 377 us; the launch traced here: 375 us
  waiting for transfers between devices  250 us (66%)
  local copies, waits for them, and re-layouts  44.8 us (12%)
  matrix products  31.4 us (8%)
  starting transfers between devices  21.2 us (6%)
  between operations  14.2 us (4%)
  other arithmetic  13.5 us (4%)
    reduce_scatter x1, waiting for transfers between devices, local(): lax.psum_scatter(partial_core, 'wide', scatter_dimension=3, tiled=True)  188 us
    all_to_all x1, waiting for transfers between devices, local(): lax.all_to_all(arrange(out_grads), ('wide', 'narrow'), split_axis=2, conc...  29.5 us
    reshape x2, local copies, waits for them, and re-layouts, arrange(): source.reshape(2, sample_rows, wide_count * narrow_count * local_modes, w...  28 us
    all_to_all x1, waiting for transfers between devices, local(): lax.all_to_all(jnp.stack([core_step] * lax.axis_size('wide')), 'wide', 0, 0)  18.1 us
    all_to_all x1, waiting for transfers between devices, local(): lax.all_to_all(arrange(spectra), ('wide', 'narrow'), split_axis=2, concat...  14.4 us
    all_to_all x1, starting transfers between devices, local(): lax.all_to_all(arrange(spectra), ('wide', 'narrow'), split_axis=2, concat...  11.2 us
    sub x1, other arithmetic, local(): new_weights = weights - 0.3 * change  10.6 us
    dot_general x1, matrix products, local(): jnp.einsum('ia,pmao->pmio', in_factor, left_part, precision=highest)  9.08 us
  transfers between devices with their start and end apart: 4, of which 4 were waited for; matrix products, arithmetic and copies ran while one was open for 5% of the time, Pallas kernels for 0%

profile of v1, /device:TPU:0, one launch (start us, length us, event | category | flops | bytes accessed | tf_op | source)
XLA Modules:
  0.0 375.3 jit_solution(3452709790436360612)
XLA Ops:
  7.2 0.0 copy-start
  7.2 1.8 copy.52
  9.0 14.0 %copy.53 = bf16[2,1,2048,256]{3,0,1,2:T(2,128)(2,1)} copy(bf16[2,1,2048,256]{3,2,0,1:T(8,128)(2,1)S(1)} %bitcast.83) | data formatting | bytes 4194304 | tf_op jit(solution)/shard_map/reshape | solution.py:31
  23.0 11.2 %all-to-all-start.1 = ((bf16[2,1,2048,256]{3,0,1,2:T(2,128)(2,1)}), bf16[2,1,2048,256]{3,0,1,2:T(2,128)(2,1)S(1)}, u32[]{:S(2)}, u32[]{:S(2)}) async-start(bf16[2,1,2048,256]{3,0,1,2:T(2,128)(2,1)} %copy.53), calls=%async_computation.1 | async-start | bytes 4194304 | tf_op jit(solution)/shard_map/all_to_all | solution.py:34
  34.2 1.8 copy.49
  36.0 14.0 %copy.50 = bf16[2,1,2048,256]{3,0,1,2:T(2,128)(2,1)} copy(bf16[2,1,2048,256]{3,2,0,1:T(8,128)(2,1)S(1)} %bitcast.84) | data formatting | bytes 4194304 | tf_op jit(solution)/shard_map/reshape | solution.py:31
  49.9 14.4 %all-to-all-done.1 = bf16[2,1,2048,256]{3,0,1,2:T(2,128)(2,1)S(1)} async-done(((bf16[2,1,2048,256]{3,0,1,2:T(2,128)(2,1)}), bf16[2,1,2048,256]{3,0,1,2:T(2,128)(2,1)S(1)}, u32[]{:S(2)}, u32[]{:S(2)}) %all-to-all-start.1) | async-done | bytes 2097184 | tf_op jit(solution)/shard_map/all_to_all | solution.py:34
  64.3 5.8 %all-to-all-start = ((bf16[2,1,2048,256]{3,0,1,2:T(2,128)(2,1)}), bf16[2,1,2048,256]{3,0,1,2:T(2,128)(2,1)}, u32[]{:S(2)}, u32[]{:S(2)}) async-start(bf16[2,1,2048,256]{3,0,1,2:T(2,128)(2,1)} %copy.50), calls=%async_computation | async-start | bytes 4194304 | tf_op jit(solution)/shard_map/all_to_all | solution.py:37
  70.1 0.2 reduce-scatter.2.cloned.1.call-start
  70.3 29.5 %all-to-all-done = bf16[2,1,2048,256]{3,0,1,2:T(2,128)(2,1)} async-done(((bf16[2,1,2048,256]{3,0,1,2:T(2,128)(2,1)}), bf16[2,1,2048,256]{3,0,1,2:T(2,128)(2,1)}, u32[]{:S(2)}, u32[]{:S(2)}) %all-to-all-start) | async-done | bytes 2097184 | tf_op jit(solution)/shard_map/all_to_all | solution.py:37
  99.8 7.4 %convolution_bitcast_fusion = f32[2,2,16,256,256]{3,4,0,1,2:T(8,128)S(1)} fusion(bf16[2,128,16,256,1]{3,0,2,1,4:T(2,128)(2,1)S(1)} %bitcast.82, bf16[2,128,16,256,1]{3,0,2,1,4:T(2,128)(2,1)} %bitcast.4), kind=kOutput, calls=%fused_computation | convolution fusion | flops 1073741824 | bytes 20971520 | tf_op jit(solution)/shard_map/pbmi,qbmo->pqmio/dot_general | solution.py:41
  107.2 0.6 fusion.4
  107.8 0.0 copy-start.1
  107.8 0.6 fusion.6
  108.4 0.2 copy-done.1
  108.6 5.6 %fusion = f32[2,16,256,64]{2,3,1,0:T(8,128)S(1)} fusion(f32[1,16,256,256]{2,3,1,0:T(8,128)S(1)} %fusion.4, f32[1,16,256,256]{2,3,1,0:T(8,128)S(1)} %fusion.6, f32[256,64]{0,1:T(8,128)S(1)} %copy-done.1), kind=kOutput, calls=%fused_computation.1 | convolution fusion | flops 1612709888 | bytes 10551296 | tf_op jit(solution)/shard_map/pmio,oc->pmic/dot_general | solution.py:45
  114.2 0.0 copy-done
  114.2 2.0 convolution_bitcast_fusion.3
  116.3 0.0 copy-start.4
  116.3 0.3 copy.60
  116.6 0.4 reshape.87
  117.0 0.0 copy-done.4
  117.0 0.0 copy-start.3
  117.0 0.0 copy-start.2
  117.0 3.5 convolution_bitcast_fusion.1
  120.5 0.0 reduce-scatter.2.cloned.1.call-update
  120.6 188.3 %reduce-scatter.2.cloned.1.call-done = f32[2,8,8,128]{3,1,2,0:T(8,128)} async-done(((f32[2,8,8,4096]{3,1,2,0:T(8,128)}), f32[2,8,8,128]{3,1,2,0:T(8,128)}) %reduce-scatter.2.cloned.1.call-update) | async-done | bytes 65552 | tf_op jit(solution)/shard_map/reduce_scatter | solution.py:51
  308.8 0.0 copy-done.3
  308.8 0.8 sqrt_add_fusion
  309.6 0.0 copy-done.2
  309.7 0.9 broadcast_divide_fusion
  310.5 1.6 stack.5
  312.1 4.0 %all-to-all-start.2 = ((f32[32,2,8,8,128]{4,2,3,1,0:T(8,128)}), f32[32,2,8,8,128]{4,2,3,1,0:T(8,128)S(1)}, u32[]{:S(2)}, u32[]{:S(2)}) async-start(f32[32,2,8,8,128]{4,2,3,1,0:T(8,128)} %stack.5), calls=%async_computation.3 | async-start | bytes 4194304 | tf_op jit(solution)/shard_map/all_to_all | solution.py:63
  316.1 0.6 copy.68
  316.7 0.6 copy.67
  317.4 18.1 %all-to-all-done.2 = f32[32,2,8,8,128]{4,2,3,1,0:T(8,128)S(1)} async-done(((f32[32,2,8,8,128]{4,2,3,1,0:T(8,128)}), f32[32,2,8,8,128]{4,2,3,1,0:T(8,128)S(1)}, u32[]{:S(2)}, u32[]{:S(2)}) %all-to-all-start.2) | async-done | bytes 2097184 | tf_op jit(solution)/shard_map/all_to_all | solution.py:63
  335.5 2.0 convolution_bitcast_fusion.2
  337.5 0.3 copy.65
  337.8 0.4 reshape.90
  338.2 1.9 fusion.14
  340.0 9.1 %broadcast_multiply_fusion = f32[2,16,256,256]{3,2,1,0:T(8,128)} fusion(f32[2,16,64,256]{3,2,1,0:T(8,128)S(1)} %fusion.14, f32[256,64]{0,1:T(8,128)S(1)} %copy-done), kind=kOutput, calls=%fused_computation.13 | convolution fusion | flops 1612709888 | bytes 10551296 | tf_op jit(solution)/shard_map/ia,pmao->pmio/dot_general | solution.py:69
  349.1 8.7 %copy.66 = f32[2,2,8,256,256]{4,3,2,1,0:T(8,128)} copy(f32[2,2,8,256,256]{3,4,2,1,0:T(8,128)} %bitcast.81) | data formatting | bytes 16777216 | tf_op jit(solution)/shard_map/mul | solution.py:71
  357.8 10.6 %sub.18 = f32[2,2,8,256,256]{4,3,2,1,0:T(8,128)} subtract(f32[2,2,8,256,256]{4,3,2,1,0:T(8,128)} %param.10, f32[2,2,8,256,256]{4,3,2,1,0:T(8,128)} %copy.66) | non-fusion elementwise | flops 2097152 | bytes 25165824 | tf_op jit(solution)/shard_map/sub | solution.py:71
Async XLA Ops:
  7.2 107.1 %copy-start = (f32[256,64]{0,1:T(8,128)S(1)}, f32[256,64]{0,1:T(8,128)}, u32[]{:S(2)}) copy-start(f32[256,64]{0,1:T(8,128)} %param.12) | copy-start | bytes 196612
  23.0 41.3 %all-to-all-start.1 = ((bf16[2,1,2048,256]{3,0,1,2:T(2,128)(2,1)}), bf16[2,1,2048,256]{3,0,1,2:T(2,128)(2,1)S(1)}, u32[]{:S(2)}, u32[]{:S(2)}) async-start(bf16[2,1,2048,256]{3,0,1,2:T(2,128)(2,1)} %copy.53), calls=%async_computation.1 | async-start | bytes 4194304 | tf_op jit(solution)/shard_map/all_to_all | solution.py:34
  64.3 35.5 %all-to-all-start = ((bf16[2,1,2048,256]{3,0,1,2:T(2,128)(2,1)}), bf16[2,1,2048,256]{3,0,1,2:T(2,128)(2,1)}, u32[]{:S(2)}, u32[]{:S(2)}) async-start(bf16[2,1,2048,256]{3,0,1,2:T(2,128)(2,1)} %copy.50), calls=%async_computation | async-start | bytes 4194304 | tf_op jit(solution)/shard_map/all_to_all | solution.py:37
  70.1 238.7 %reduce-scatter.2.cloned.1.call-start = ((), (), s32[]{:S(2)}) async-start(), calls=%async_computation.4 | async-start | bytes 2162688 | tf_op jit(solution)/shard_map/reduce_scatter | solution.py:51
  107.8 0.8 copy-start.1
  116.3 0.7 copy-start.4
  117.0 191.9 %copy-start.3 = (f32[8,8,128]{2,1,0:T(8,128)S(1)}, f32[8,8,128]{2,1,0:T(8,128)}, u32[]{:S(2)}) copy-start(f32[8,8,128]{2,1,0:T(8,128)} %param.15) | copy-start | bytes 98308
  117.0 192.6 %copy-start.2 = (f32[2,8,8,128]{3,2,1,0:T(8,128)S(1)}, f32[2,8,8,128]{3,2,1,0:T(8,128)}, u32[]{:S(2)}) copy-start(f32[2,8,8,128]{3,2,1,0:T(8,128)} %param.14) | copy-start | bytes 196612
  312.1 23.4 %all-to-all-start.2 = ((f32[32,2,8,8,128]{4,2,3,1,0:T(8,128)}), f32[32,2,8,8,128]{4,2,3,1,0:T(8,128)S(1)}, u32[]{:S(2)}, u32[]{:S(2)}) async-start(f32[32,2,8,8,128]{4,2,3,1,0:T(8,128)} %stack.5), calls=%async_computation.3 | async-start | bytes 4194304 | tf_op jit(solution)/shard_map/all_to_all | solution.py:63
Sparse Core Ops, SparseCore 0:
  120.7 188.1 reduce-scatter.1
